TPU v7x, 32 devices: a whole 2x2x4 slice. The times are simulated.
32 devices in a mesh: dp: 2 (over y), ctx: 4 (over x, core), tensor: 4 (over z).
Axes of the slice: x: 2, y: 2, z: 4, core: 2. Of those that a mesh axis runs over, the one named last changes fastest.
Arguments:
- hidden: bfloat16 [4, 1024, 2048], P('dp', 'ctx'), may hold values from -6 to 6
- cotangent: bfloat16 [4, 1024, 2048], P('dp', 'ctx'), may hold values from -6 to 6
- segment_ids: int32 [4, 1024], P('dp', 'ctx'), may hold values from 0 to 5, never falling along the last dimension, each value on 1 to 800 neighbouring positions
- attn_gain: bfloat16 [2048], P(('dp', 'ctx')), may hold values from 0.5 to 1.5
- w_query: bfloat16 [2048, 2048], P(('dp', 'ctx'), 'tensor'), may hold values from -0.125 to 0.125
- key_matrix: bfloat16 [2048, 256], P(('dp', 'ctx'), 'tensor'), may hold values from -0.125 to 0.125
- value_matrix: bfloat16 [2048, 256], P(('dp', 'ctx'), 'tensor'), may hold values from -0.125 to 0.125
- w_out: bfloat16 [2048, 2048], P('tensor', ('dp', 'ctx')), may hold values from -1 to 1
- mlp_gain: bfloat16 [2048], P(('dp', 'ctx')), may hold values from 0.5 to 1.5
- w_gate: bfloat16 [2048, 5632], P(('dp', 'ctx'), 'tensor'), may hold values from -0.125 to 0.125
- w_up: bfloat16 [2048, 5632], P(('dp', 'ctx'), 'tensor'), may hold values from -0.125 to 0.125
- w_down: bfloat16 [5632, 2048], P('tensor', ('dp', 'ctx')), may hold values from -0.078125 to 0.078125
Outputs:
- layer_out: bfloat16 [4, 1024, 2048], P('dp', 'ctx')
- d_hidden: float32 [4, 1024, 2048], P('dp', 'ctx')
- grad_attn_gain: float32 [2048], P(('dp', 'ctx'))
- grad_query: float32 [2048, 2048], P(('dp', 'ctx'), 'tensor')
- grad_key: float32 [2048, 256], P(('dp', 'ctx'), 'tensor')
- grad_value: float32 [2048, 256], P(('dp', 'ctx'), 'tensor')
- grad_out: float32 [2048, 2048], P('tensor', ('dp', 'ctx'))
- grad_mlp_gain: float32 [2048], P(('dp', 'ctx'))
- grad_gate: float32 [2048, 5632], P(('dp', 'ctx'), 'tensor')
- grad_up: float32 [2048, 5632], P(('dp', 'ctx'), 'tensor')
- grad_down: float32 [5632, 2048], P('tensor', ('dp', 'ctx'))
Inputs may be any that keep to these rules, and one draw needn't show every extreme that they name: `segment_ids`: along each sequence the ids never fall, every id appears, each document holds 1 to 800 tokens, and one holds exactly 800.
All inputs are finite; a program needn't handle non-finite values.
Results may differ from a plain program's by a relative error of at most 0.013.
Values may be sent and summed in bfloat16 or wider, within the bound.
No kernel may reach another device: no remote copies, remote signals or barrier semaphores. Data moves between devices by JAX's collectives and lax.ppermute only.
A program may use at most 192 MiB of HBM per device.

v0:
```python
import jax
import jax.numpy as jnp
from jax import lax
from jax.sharding import PartitionSpec as P

MB = 2
EPSILON = 1e-05
THETA = 10000.0
NEG_FILL = -1e30


def inv_rms(values):
    return lax.rsqrt(jnp.mean(values * values, axis=-1, keepdims=True) + EPSILON)


def angles_for(positions, head_size):
    freq_index = jnp.arange(head_size // 2, dtype=jnp.float32)
    inverse = jnp.power(jnp.float32(THETA), -2.0 * freq_index / head_size)
    angle_table = positions.astype(jnp.float32)[:, None] * inverse[None, :]
    return (jnp.cos(angle_table), jnp.sin(angle_table))


def rotary(vectors, cosine, sine_table):
    half_size = vectors.shape[-1] // 2
    front_half = vectors[..., :half_size]
    back_half = vectors[..., half_size:]
    return jnp.concatenate(
        [
            front_half * cosine - back_half * sine_table,
            back_half * cosine + front_half * sine_table,
        ],
        axis=-1,
    )


def norm_back(grad_normed, source, inv_scale, gain_full):
    normalized = source * inv_scale
    scaled = grad_normed * gain_full
    middle = jnp.mean(scaled * normalized, axis=-1, keepdims=True)
    gain_term = jnp.sum(grad_normed * normalized, axis=(0, 1))
    return (inv_scale * (scaled - normalized * middle), gain_term)


def collect(shards):
    return (
        lax.all_gather(shards[0], ("dp", "ctx"), axis=0, tiled=True),
        lax.all_gather(shards[1], ("dp", "ctx"), axis=0, tiled=True),
        lax.all_gather(shards[2], ("dp", "ctx"), axis=0, tiled=True),
        lax.all_gather(shards[3], ("dp", "ctx"), axis=0, tiled=True),
        lax.all_gather(shards[4], ("dp", "ctx"), axis=1, tiled=True),
        lax.all_gather(shards[5], ("dp", "ctx"), axis=0, tiled=True),
        lax.all_gather(shards[6], ("dp", "ctx"), axis=0, tiled=True),
        lax.all_gather(shards[7], ("dp", "ctx"), axis=0, tiled=True),
        lax.all_gather(shards[8], ("dp", "ctx"), axis=1, tiled=True),
    )


def contract(left_side, right_side):
    return jnp.einsum("stc,stf->cf", left_side, right_side, preferred_element_type=jnp.float32)


def project_back(grad_rows, weight_full):
    return jnp.einsum("stf,cf->stc", grad_rows, weight_full, preferred_element_type=jnp.float32)


def per_device(
    hidden,
    cotangent,
    segment_ids,
    attn_gain,
    w_query,
    key_matrix,
    value_matrix,
    w_out,
    mlp_gain,
    w_gate,
    w_up,
    w_down,
):
    shards = (attn_gain, w_query, key_matrix, value_matrix, w_out, mlp_gain, w_gate, w_up, w_down)
    span_len = hidden.shape[1]
    model_width = hidden.shape[2]
    seq_count = hidden.shape[0] // MB
    head_size = key_matrix.shape[1]
    local_heads = w_query.shape[1] // head_size
    seq_len = span_len * lax.axis_size("ctx")
    score_scale = head_size ** (-0.5)
    positions_q = lax.axis_index("ctx") * span_len + jnp.arange(span_len, dtype=jnp.int32)
    positions_k = jnp.arange(seq_len, dtype=jnp.int32)
    cosine, sine_table = angles_for(positions_q, head_size)
    cos_heads = cosine[:, None, :]
    sin_heads = sine_table[:, None, :]
    causal = positions_q[:, None] >= positions_k[None, :]
    grad_list = [
        jnp.zeros((model_width,), jnp.float32),
        jnp.zeros((model_width, w_query.shape[1]), jnp.float32),
        jnp.zeros((model_width, key_matrix.shape[1]), jnp.float32),
        jnp.zeros((model_width, value_matrix.shape[1]), jnp.float32),
        jnp.zeros((w_out.shape[0], model_width), jnp.float32),
        jnp.zeros((model_width,), jnp.float32),
        jnp.zeros((model_width, w_gate.shape[1]), jnp.float32),
        jnp.zeros((model_width, w_up.shape[1]), jnp.float32),
        jnp.zeros((w_down.shape[0], model_width), jnp.float32),
    ]
    outputs = []
    input_grads = []
    for batch_index in range(MB):
        gathered = collect(shards)
        gain_one, query_w, key_w, value_w, out_w, gain_two, gate_w, up_w, down_w = gathered
        gain_one = gain_one.astype(jnp.float32)
        gain_two = gain_two.astype(jnp.float32)
        row_range = slice(batch_index * seq_count, (batch_index + 1) * seq_count)
        source = hidden[row_range].astype(jnp.float32)
        seg_local = segment_ids[row_range]
        inv_one = inv_rms(source)
        first_normalized = (source * inv_one * gain_one).astype(jnp.bfloat16)
        query_proj = jnp.dot(first_normalized, query_w, preferred_element_type=jnp.float32)
        projected_keys = jnp.dot(first_normalized, key_w, preferred_element_type=jnp.float32)
        projected_values = jnp.dot(first_normalized, value_w, preferred_element_type=jnp.float32)
        query_rows = rotary(
            query_proj.reshape(seq_count, span_len, local_heads, head_size), cos_heads, sin_heads
        ).astype(jnp.bfloat16)
        keys_local = rotary(projected_keys, cosine, sine_table).astype(jnp.bfloat16)
        values_local = projected_values.astype(jnp.bfloat16)
        keys_all, values_all, seg_all = (
            lax.all_gather(keys_local, "ctx", axis=1, tiled=True),
            lax.all_gather(values_local, "ctx", axis=1, tiled=True),
            lax.all_gather(seg_local.astype(jnp.bfloat16), "ctx", axis=1, tiled=True),
        )
        allowed = (seg_local[:, :, None] == seg_all.astype(jnp.int32)[:, None, :]) & causal[None]
        allowed = allowed[:, None]
        logits = (
            jnp.einsum("sqhd,skd->shqk", query_rows, keys_all, preferred_element_type=jnp.float32)
            * score_scale
        )
        logits = jnp.where(allowed, logits, NEG_FILL)
        row_peak = jnp.max(logits, axis=-1, keepdims=True)
        shifted = jnp.exp(logits - row_peak)
        totals = jnp.sum(shifted, axis=-1, keepdims=True)
        probs_low = (shifted / totals).astype(jnp.bfloat16)
        log_norm = row_peak + jnp.log(totals)
        heads_out = jnp.einsum(
            "shqk,skd->sqhd", probs_low, values_all, preferred_element_type=jnp.float32
        )
        heads_out = heads_out.reshape(seq_count, span_len, local_heads * head_size).astype(
            jnp.bfloat16
        )
        attn_out = lax.psum(jnp.dot(heads_out, out_w, preferred_element_type=jnp.float32), "tensor")
        residual = source + attn_out
        inv_two = inv_rms(residual)
        normed_two = (residual * inv_two * gain_two).astype(jnp.bfloat16)
        gate_pre = jnp.dot(normed_two, gate_w, preferred_element_type=jnp.float32)
        up_pre = jnp.dot(normed_two, up_w, preferred_element_type=jnp.float32)
        gate_sigmoid = jax.nn.sigmoid(gate_pre)
        silu_gate = gate_pre * gate_sigmoid
        activated = (silu_gate * up_pre).astype(jnp.bfloat16)
        mlp_out = lax.psum(
            jnp.dot(activated, down_w, preferred_element_type=jnp.float32).astype(jnp.bfloat16),
            "tensor",
        ).astype(jnp.float32)
        outputs.append((residual + mlp_out).astype(jnp.bfloat16))
        grad_top = cotangent[row_range]
        grad_list[8] = grad_list[8] + contract(activated, grad_top)
        d_act = project_back(grad_top, down_w)
        d_gate = (d_act * up_pre * gate_sigmoid * (1.0 + gate_pre * (1.0 - gate_sigmoid))).astype(
            jnp.bfloat16
        )
        d_up = (d_act * silu_gate).astype(jnp.bfloat16)
        grad_list[6] = grad_list[6] + contract(normed_two, d_gate)
        grad_list[7] = grad_list[7] + contract(normed_two, d_up)
        mlp_partial = project_back(d_gate, gate_w) + project_back(d_up, up_w)
        d_normed_two = lax.psum(mlp_partial, "tensor")
        d_norm_two, gain_term_two = norm_back(d_normed_two, residual, inv_two, gain_two)
        d_residual = grad_top.astype(jnp.float32) + d_norm_two
        d_residual_low = d_residual.astype(jnp.bfloat16)
        grad_list[5] = grad_list[5] + gain_term_two
        grad_list[4] = grad_list[4] + contract(heads_out, d_residual_low)
        d_heads = project_back(d_residual_low, out_w).astype(jnp.bfloat16)
        d_heads = d_heads.reshape(seq_count, span_len, local_heads, head_size)
        again = (
            jnp.einsum("sqhd,skd->shqk", query_rows, keys_all, preferred_element_type=jnp.float32)
            * score_scale
        )
        again = jnp.where(allowed, again, NEG_FILL)
        probs_again = jnp.exp(again - log_norm)
        probs_again_low = probs_again.astype(jnp.bfloat16)
        d_probs = jnp.einsum(
            "sqhd,skd->shqk", d_heads, values_all, preferred_element_type=jnp.float32
        )
        row_delta = jnp.sum(probs_again * d_probs, axis=-1, keepdims=True)
        d_scores = (probs_again * (d_probs - row_delta)).astype(jnp.bfloat16)
        d_query = (
            jnp.einsum("shqk,skd->sqhd", d_scores, keys_all, preferred_element_type=jnp.float32)
            * score_scale
        )
        key_terms = (
            jnp.einsum("shqk,sqhd->ksd", d_scores, query_rows, preferred_element_type=jnp.float32)
            * score_scale
        )
        value_terms = jnp.einsum(
            "shqk,sqhd->ksd", probs_again_low, d_heads, preferred_element_type=jnp.float32
        )
        kv_terms = jnp.stack([key_terms, value_terms], axis=1).reshape(
            seq_len, 2 * seq_count * head_size
        )
        kv_local = lax.psum_scatter(kv_terms, "ctx", scatter_dimension=0, tiled=True).reshape(
            span_len, 2, seq_count, head_size
        )
        d_key = jnp.transpose(kv_local[:, 0], (1, 0, 2))
        d_value = jnp.transpose(kv_local[:, 1], (1, 0, 2))
        d_query_proj = rotary(d_query, cos_heads, -sin_heads).astype(jnp.bfloat16)
        d_query_proj = d_query_proj.reshape(seq_count, span_len, local_heads * head_size)
        d_key_proj = rotary(d_key, cosine, -sine_table).astype(jnp.bfloat16)
        d_value_proj = d_value.astype(jnp.bfloat16)
        grad_list[1] = grad_list[1] + contract(first_normalized, d_query_proj)
        grad_list[2] = grad_list[2] + contract(first_normalized, d_key_proj)
        grad_list[3] = grad_list[3] + contract(first_normalized, d_value_proj)
        attn_partial = (
            project_back(d_query_proj, query_w)
            + project_back(d_key_proj, key_w)
            + project_back(d_value_proj, value_w)
        )
        d_normed_one = lax.psum(attn_partial, "tensor")
        d_norm_one, gain_term_one = norm_back(d_normed_one, source, inv_one, gain_one)
        grad_list[0] = grad_list[0] + gain_term_one
        input_grads.append(d_residual + d_norm_one)
    input_grad_rows = jnp.concatenate(input_grads, axis=0)
    summed = (
        lax.psum_scatter(grad_list[0], ("dp", "ctx"), scatter_dimension=0, tiled=True),
        lax.psum_scatter(grad_list[1], ("dp", "ctx"), scatter_dimension=0, tiled=True),
        lax.psum_scatter(grad_list[2], ("dp", "ctx"), scatter_dimension=0, tiled=True),
        lax.psum_scatter(grad_list[3], ("dp", "ctx"), scatter_dimension=0, tiled=True),
        lax.psum_scatter(grad_list[4], ("dp", "ctx"), scatter_dimension=1, tiled=True),
        lax.psum_scatter(grad_list[5], ("dp", "ctx"), scatter_dimension=0, tiled=True),
        lax.psum_scatter(grad_list[6], ("dp", "ctx"), scatter_dimension=0, tiled=True),
        lax.psum_scatter(grad_list[7], ("dp", "ctx"), scatter_dimension=0, tiled=True),
        lax.psum_scatter(grad_list[8], ("dp", "ctx"), scatter_dimension=1, tiled=True),
    )
    return (
        jnp.concatenate(outputs, axis=0),
        input_grad_rows,
        summed[0],
        summed[1],
        summed[2],
        summed[3],
        summed[4],
        summed[5],
        summed[6],
        summed[7],
        summed[8],
    )


def solution(mesh):
    in_specs = (
        P("dp", "ctx", None),
        P("dp", "ctx", None),
        P("dp", "ctx"),
        P(("dp", "ctx")),
        P(("dp", "ctx"), "tensor"),
        P(("dp", "ctx"), "tensor"),
        P(("dp", "ctx"), "tensor"),
        P("tensor", ("dp", "ctx")),
        P(("dp", "ctx")),
        P(("dp", "ctx"), "tensor"),
        P(("dp", "ctx"), "tensor"),
        P("tensor", ("dp", "ctx")),
    )
    out_specs = (
        P("dp", "ctx", None),
        P("dp", "ctx", None),
        P(("dp", "ctx")),
        P(("dp", "ctx"), "tensor"),
        P(("dp", "ctx"), "tensor"),
        P(("dp", "ctx"), "tensor"),
        P("tensor", ("dp", "ctx")),
        P(("dp", "ctx")),
        P(("dp", "ctx"), "tensor"),
        P(("dp", "ctx"), "tensor"),
        P("tensor", ("dp", "ctx")),
    )
    return jax.shard_map(
        per_device, mesh=mesh, in_specs=in_specs, out_specs=out_specs, check_vma=False
    )
```

profile of v0, /device:TPU:0, one launch (start us, length us, event | category | flops | bytes accessed | tf_op | source)
XLA Modules:
  0.0 1380.9 jit_solution(2608815866896692798)
XLA Ops:
  11.5 10.4 all-gather.2
  22.0 9.8 all_gather.58
  32.9 9.8 all_gather.55
  102.9 9.4 all-gather.3
  112.3 144.4 %all-reduce.16.cloned.1.call-done = (f32[1,256,2048]{2,1,0:T(8,128)}, f32[1,256,2048]{2,1,0:T(8,128)}) async-done(((f32[1,256,2048]{2,1,0:T(8,128)}, f32[1,256,2048]{2,1,0:T(8,128)}), (f32[1,256,2048]{2,1,0:T(8,128)}, f32[1,256,2048]{2,1,0:T(8,128)})) %all-reduce.16.cloned.1.call-update) | async-done | bytes 4194320 | tf_op jit(solution)/shard_map/psum | solution.py:148
  262.9 37.8 %all-gather.16.cloned.1.call-done = bf16[2048,1408]{1,0:T(8,128)(2,1)} async-done(((bf16[256,1408]{1,0:T(8,128)(2,1)}), bf16[2048,1408]{1,0:T(8,128)(2,1)}) %all-gather.16.cloned.1.call-update) | async-done | bytes 5767184 | tf_op jit(solution)/shard_map/all_gather | solution.py:53
  306.5 39.1 %all-gather.14.cloned.1.call-done = bf16[2048,1408]{1,0:T(8,128)(2,1)} async-done(((bf16[256,1408]{1,0:T(8,128)(2,1)}), bf16[2048,1408]{1,0:T(8,128)(2,1)}) %all-gather.14.cloned.1.call-update) | async-done | bytes 5767184 | tf_op jit(solution)/shard_map/all_gather | solution.py:52
  357.5 34.2 %all-gather.18.cloned.1.call-done = bf16[1408,2048]{1,0:T(8,128)(2,1)} async-done(((bf16[1408,256]{1,0:T(8,128)(2,1)}), bf16[1408,2048]{1,0:T(8,128)(2,1)}) %all-gather.18.cloned.1.call-update) | async-done | bytes 5767184 | tf_op jit(solution)/shard_map/all_gather | solution.py:54
  391.6 7.1 multiply_convert_fusion.2
  429.2 142.4 %all-reduce.14.cloned.1.call-done = (f32[1,256,2048]{2,1,0:T(8,128)}, f32[1,256,2048]{2,1,0:T(8,128)}) async-done(((f32[1,256,2048]{2,1,0:T(8,128)}, f32[1,256,2048]{2,1,0:T(8,128)}), (f32[1,256,2048]{2,1,0:T(8,128)}, f32[1,256,2048]{2,1,0:T(8,128)})) %all-reduce.14.cloned.1.call-update) | async-done | bytes 4194320 | tf_op jit(solution)/shard_map/psum | solution.py:172
  576.6 83.1 %all-reduce.18.cloned.1.call-done = (bf16[1,256,2048]{2,1,0:T(8,128)(2,1)}, bf16[1,256,2048]{2,1,0:T(8,128)(2,1)}) async-done(((bf16[1,256,2048]{2,1,0:T(8,128)(2,1)}, bf16[1,256,2048]{2,1,0:T(8,128)(2,1)}), (bf16[1,256,2048]{2,1,0:T(8,128)(2,1)}, bf16[1,256,2048]{2,1,0:T(8,128)(2,1)})) %all-reduce.18.cloned.1.call-update) | async-done | bytes 2097168 | tf_op jit(solution)/shard_map/psum | solution.py:157
  659.8 7.3 multiply_add_fusion.1
  676.6 8.8 fusion
  693.6 8.9 fusion.3
  707.5 7.0 fusion.16
  728.9 23.7 %reduce-scatter.10.cloned.1.call-done = f32[256,128]{0,1:T(8,128)} async-done(((f32[1024,128]{0,1:T(8,128)}), f32[256,128]{0,1:T(8,128)}) %reduce-scatter.10.cloned.1.call-update) | async-done | bytes 131088 | tf_op jit(solution)/shard_map/reduce_scatter | solution.py:206
  810.9 105.5 %all-reduce.12.cloned.1.call-done = (f32[1,256,2048]{2,1,0:T(8,128)}, f32[1,256,2048]{2,1,0:T(8,128)}) async-done(((f32[1,256,2048]{2,1,0:T(8,128)}, f32[1,256,2048]{2,1,0:T(8,128)}), (f32[1,256,2048]{2,1,0:T(8,128)}, f32[1,256,2048]{2,1,0:T(8,128)})) %all-reduce.12.cloned.1.call-update) | async-done | bytes 4194320 | tf_op jit(solution)/shard_map/psum | solution.py:223
  919.7 23.9 %all-reduce.2 = (f32[2048]{0:T(1024)S(1)}, f32[2048]{0:T(1024)S(1)}) all-reduce(f32[2048]{0:T(1024)S(1)} %add.260, f32[2048]{0:T(1024)S(1)} %add.265), channel_id=6, replica_groups=mesh['dp'=2,'ctx'=4,'tensor'=4] {'dp','ctx'}, use_global_device_ids=true, to_apply=%region_26.27.clone | all-reduce | flops 4096 | bytes 32768
  953.0 37.8 %reduce-scatter.18.cloned.1.call-done = f32[256,64]{0,1:T(8,128)} async-done(((f32[2048,64]{0,1:T(8,128)}), f32[256,64]{0,1:T(8,128)}) %reduce-scatter.18.cloned.1.call-update) | async-done | bytes 65552 | tf_op jit(solution)/shard_map/reduce_scatter | solution.py:232
  990.8 54.9 %reduce-scatter.20.cloned.1.call-done = f32[512,256]{1,0:T(8,128)} async-done(((f32[512,2048]{1,0:T(8,128)}), f32[512,256]{1,0:T(8,128)}) %reduce-scatter.20.cloned.1.call-update) | async-done | bytes 524304 | tf_op jit(solution)/shard_map/reduce_scatter | solution.py:233
  1045.7 55.0 %reduce-scatter.14.cloned.1.call-done = f32[256,512]{1,0:T(8,128)} async-done(((f32[2048,512]{1,0:T(8,128)}), f32[256,512]{1,0:T(8,128)}) %reduce-scatter.14.cloned.1.call-update) | async-done | bytes 524304 | tf_op jit(solution)/shard_map/reduce_scatter | solution.py:230
  1100.7 91.1 %reduce-scatter.24.cloned.1.call-done = f32[256,1408]{1,0:T(8,128)} async-done(((f32[2048,1408]{1,0:T(8,128)}), f32[256,1408]{1,0:T(8,128)}) %reduce-scatter.24.cloned.1.call-update) | async-done | bytes 1441808 | tf_op jit(solution)/shard_map/reduce_scatter | solution.py:236
  1191.8 91.1 %reduce-scatter.22.cloned.1.call-done = f32[256,1408]{1,0:T(8,128)} async-done(((f32[2048,1408]{1,0:T(8,128)}), f32[256,1408]{1,0:T(8,128)}) %reduce-scatter.22.cloned.1.call-update) | async-done | bytes 1441808 | tf_op jit(solution)/shard_map/reduce_scatter | solution.py:235
  1282.9 90.8 %reduce-scatter.26.cloned.1.call-done = f32[1408,256]{1,0:T(8,128)} async-done(((f32[1408,2048]{1,0:T(8,128)}), f32[1408,256]{1,0:T(8,128)}) %reduce-scatter.26.cloned.1.call-update) | async-done | bytes 1441808 | tf_op jit(solution)/shard_map/reduce_scatter | solution.py:237
  (362 shorter events, 230.9 us)
Async XLA Ops:
  7.2 71.3 %all-gather.10.cloned.1.call-start = ((), (), s32[]{:S(2)}) async-start(), calls=%async_computation.9 | async-start | bytes 2359296 | tf_op jit(solution)/shard_map/all_gather | solution.py:47
  7.9 87.2 %all-gather.12.cloned.1.call-start = ((), (), s32[]{:S(2)}) async-start(), calls=%async_computation.10 | async-start | bytes 2359296 | tf_op jit(solution)/shard_map/all_gather | solution.py:50
  8.7 248.0 %all-reduce.16.cloned.1.call-start = ((), (), s32[]{:S(2)}) async-start(), calls=%async_computation.25 | async-start | bytes 8388608 | tf_op jit(solution)/shard_map/psum | solution.py:148
  8.7 45.9 %copy-start.85 = (f32[32]{0:T(128)}, f32[32]{0:T(128)S(1)}, u32[]{:S(2)}) copy-start(f32[32]{0:T(128)S(1)} %multiply_power_fusion) | copy-start | bytes 388
  8.8 45.9 %copy-start.83 = (f32[256]{0:T(256)}, f32[256]{0:T(256)S(1)}, u32[]{:S(2)}) copy-start(f32[256]{0:T(256)S(1)} %fusion.169) | copy-start | bytes 3076
  11.5 73.5 %copy-start.79 = (f32[256]{0:T(256)}, f32[256]{0:T(256)S(1)}, u32[]{:S(2)}) copy-start(f32[256]{0:T(256)S(1)} %add_rsqrt_fusion.3) | copy-start | bytes 3076
  11.5 70.9 %copy-start.81 = (f32[256]{0:T(256)}, f32[256]{0:T(256)S(1)}, u32[]{:S(2)}) copy-start(f32[256]{0:T(256)S(1)} %add_rsqrt_fusion.1) | copy-start | bytes 3076
  101.1 199.6 %all-gather.16.cloned.1.call-start = ((), (), s32[]{:S(2)}) async-start(), calls=%async_computation.12 | async-start | bytes 6488064 | tf_op jit(solution)/shard_map/all_gather | solution.py:53
  101.6 243.9 %all-gather.14.cloned.1.call-start = ((), (), s32[]{:S(2)}) async-start(), calls=%async_computation.11 | async-start | bytes 6488064 | tf_op jit(solution)/shard_map/all_gather | solution.py:52
  102.2 289.4 %all-gather.18.cloned.1.call-start = ((), (), s32[]{:S(2)}) async-start(), calls=%async_computation.13 | async-start | bytes 6488064 | tf_op jit(solution)/shard_map/all_gather | solution.py:54
  102.8 468.8 %all-reduce.14.cloned.1.call-start = ((), (), s32[]{:S(2)}) async-start(), calls=%async_computation.24 | async-start | bytes 8388608 | tf_op jit(solution)/shard_map/psum | solution.py:172
  416.5 243.3 %all-reduce.18.cloned.1.call-start = ((), (), s32[]{:S(2)}) async-start(), calls=%async_computation.26 | async-start | bytes 4194304 | tf_op jit(solution)/shard_map/psum | solution.py:157
  427.9 300.2 %reduce-scatter.12.cloned.1.call-start = ((), (), s32[]{:S(2)}) async-start(), calls=%async_computation.15 | async-start | bytes 655360 | tf_op jit(solution)/shard_map/reduce_scatter | solution.py:206
  707.2 45.4 %reduce-scatter.10.cloned.1.call-start = ((), (), s32[]{:S(2)}) async-start(), calls=%async_computation.14 | async-start | bytes 655360 | tf_op jit(solution)/shard_map/reduce_scatter | solution.py:206
  720.1 196.2 %all-reduce.12.cloned.1.call-start = ((), (), s32[]{:S(2)}) async-start(), calls=%async_computation.23 | async-start | bytes 8388608 | tf_op jit(solution)/shard_map/psum | solution.py:223
  724.2 29.3 %copy-start.86 = (f32[32]{0:T(128)S(1)}, f32[32]{0:T(128)}, u32[]{:S(2)}) copy-start(f32[32]{0:T(128)} %copy-done.85) | copy-start | bytes 388
  724.2 30.2 %copy-start.21 = (bf16[2048,64]{0,1:T(8,128)(2,1)S(1)}, bf16[2048,64]{0,1:T(8,128)(2,1)}, u32[]{:S(2)}) copy-start(bf16[2048,64]{0,1:T(8,128)(2,1)} %copy-done.20) | copy-start | bytes 786436
  761.2 191.8 %reduce-scatter.16.cloned.1.call-start = ((), (), s32[]{:S(2)}) async-start(), calls=%async_computation.17 | async-start | bytes 589824 | tf_op jit(solution)/shard_map/reduce_scatter | solution.py:231
  763.7 227.1 %reduce-scatter.18.cloned.1.call-start = ((), (), s32[]{:S(2)}) async-start(), calls=%async_computation.18 | async-start | bytes 589824 | tf_op jit(solution)/shard_map/reduce_scatter | solution.py:232
  766.4 279.3 %reduce-scatter.20.cloned.1.call-start = ((), (), s32[]{:S(2)}) async-start(), calls=%async_computation.19 | async-start | bytes 4718592 | tf_op jit(solution)/shard_map/reduce_scatter | solution.py:233
  772.0 328.7 %reduce-scatter.14.cloned.1.call-start = ((), (), s32[]{:S(2)}) async-start(), calls=%async_computation.16 | async-start | bytes 4718592 | tf_op jit(solution)/shard_map/reduce_scatter | solution.py:230
  776.8 415.0 %reduce-scatter.24.cloned.1.call-start = ((), (), s32[]{:S(2)}) async-start(), calls=%async_computation.21 | async-start | bytes 12976128 | tf_op jit(solution)/shard_map/reduce_scatter | solution.py:236
  786.6 496.3 %reduce-scatter.22.cloned.1.call-start = ((), (), s32[]{:S(2)}) async-start(), calls=%async_computation.20 | async-start | bytes 12976128 | tf_op jit(solution)/shard_map/reduce_scatter | solution.py:235
  796.1 577.5 %reduce-scatter.26.cloned.1.call-start = ((), (), s32[]{:S(2)}) async-start(), calls=%async_computation.22 | async-start | bytes 12976128 | tf_op jit(solution)/shard_map/reduce_scatter | solution.py:237
  (98 other events, 459.1 us)
Sparse Core Ops, SparseCore 0:
  9.9 31.1 all-gather.9
  43.0 28.4 all-gather.11
  101.2 155.4 all-reduce.15
  258.4 42.1 all-gather.15
  302.4 43.1 all-gather.13
  347.3 44.2 all-gather.17
  416.6 154.9 all-reduce.13
  574.6 85.1 all-reduce.17
  707.4 20.6 reduce-scatter.11
  731.0 21.6 reduce-scatter.9
  761.3 155.0 all-reduce.11
  919.9 33.0 reduce-scatter.15
  956.6 34.1 reduce-scatter.17
  994.6 51.0 reduce-scatter.19
  1049.5 51.1 reduce-scatter.13
  1104.6 87.1 reduce-scatter.23
  1195.7 87.1 reduce-scatter.21
  1286.8 86.8 reduce-scatter.25
where the time goes:
time: 1390 us; the launch traced here: 1380 us
  waiting for transfers between devices  1040 us (75%)
  matrix products  159 us (11%)
  blocking collectives  96.4 us (7%)
  other arithmetic  48.5 us (3%)
  local copies, waits for them, and re-layouts  21.8 us (2%)
  between operations  16.7 us (1%)
    psum x1, waiting for transfers between devices, per_device(): lax.psum(jnp.dot(heads_out, out_w, preferred_element_type=jnp.float32), '...  144 us
    psum x1, waiting for transfers between devices, per_device(): d_normed_two = lax.psum(mlp_partial, 'tensor')  142 us
    psum x1, waiting for transfers between devices, per_device(): d_normed_one = lax.psum(attn_partial, 'tensor')  106 us
    reduce_scatter x1, waiting for transfers between devices, per_device(): lax.psum_scatter(grad_list[7], ('dp', 'ctx'), scatter_dimension=0, tiled=...  91.1 us
    reduce_scatter x1, waiting for transfers between devices, per_device(): lax.psum_scatter(grad_list[6], ('dp', 'ctx'), scatter_dimension=0, tiled=...  91.1 us
    reduce_scatter x1, waiting for transfers between devices, per_device(): lax.psum_scatter(grad_list[8], ('dp', 'ctx'), scatter_dimension=1, tiled=...  90.8 us
    psum x1, waiting for transfers between devices, per_device(): lax.psum(jnp.dot(activated, down_w, preferred_element_type=jnp.float32).a...  83.1 us
    reduce_scatter x1, waiting for transfers between devices, per_device(): lax.psum_scatter(grad_list[1], ('dp', 'ctx'), scatter_dimension=0, tiled=...  55 us
  transfers between devices with their start and end apart: 18, of which 16 were waited for; matrix products, arithmetic and copies ran while one was open for 10% of the time, Pallas kernels for 0%

commit v1 on v0

--- a/solution.py
+++ b/solution.py
@@ -169,7 +169,7 @@
         grad_list[6] = grad_list[6] + contract(normed_two, d_gate)
         grad_list[7] = grad_list[7] + contract(normed_two, d_up)
         mlp_partial = project_back(d_gate, gate_w) + project_back(d_up, up_w)
-        d_normed_two = lax.psum(mlp_partial, "tensor")
+        d_normed_two = jnp.sum(lax.all_gather(mlp_partial, "tensor"), axis=0)
         d_norm_two, gain_term_two = norm_back(d_normed_two, residual, inv_two, gain_two)
         d_residual = grad_top.astype(jnp.float32) + d_norm_two
         d_residual_low = d_residual.astype(jnp.bfloat16)

time: 1390 us -> 1550 us (1.12)
  waiting for transfers between devices: 1040 us -> 1170 us
  other arithmetic: 48.5 us -> 68.3 us
    all_gather x0 -> x2, waiting for transfers between devices: none -> 284 us  [per_device(): d_normed_two = jnp.sum(lax.all_gather(mlp_partial, 'tensor'), axis=0)]
    psum x1 -> x0, waiting for transfers between devices: 142 us -> none  [per_device(): d_normed_two = lax.psum(mlp_partial, 'tensor')]
  transfers between devices with their start and end apart: 18 -> 19, of which waited for: 16 -> 17; matrix products, arithmetic and copies ran while one was open for 10% -> 9% of each run, Pallas kernels for 0% -> 0%
where the time goes in v1:
time: 1550 us; the launch traced here: 1540 us
  waiting for transfers between devices  1170 us (75%)
  matrix products  164 us (11%)
  blocking collectives  96.6 us (6%)
  other arithmetic  68.3 us (4%)
  local copies, waits for them, and re-layouts  22 us (1%)
  between operations  16.1 us (1%)
    all_gather x2, waiting for transfers between devices, per_device(): d_normed_two = jnp.sum(lax.all_gather(mlp_partial, 'tensor'), axis=0)  284 us
    psum x1, waiting for transfers between devices, per_device(): lax.psum(jnp.dot(heads_out, out_w, preferred_element_type=jnp.float32), '...  144 us
    psum x1, waiting for transfers between devices, per_device(): d_normed_one = lax.psum(attn_partial, 'tensor')  96.7 us
    reduce_scatter x1, waiting for transfers between devices, per_device(): lax.psum_scatter(grad_list[7], ('dp', 'ctx'), scatter_dimension=0, tiled=...  91.1 us
    reduce_scatter x1, waiting for transfers between devices, per_device(): lax.psum_scatter(grad_list[6], ('dp', 'ctx'), scatter_dimension=0, tiled=...  91.1 us
    reduce_scatter x1, waiting for transfers between devices, per_device(): lax.psum_scatter(grad_list[8], ('dp', 'ctx'), scatter_dimension=1, tiled=...  90.8 us
    psum x1, waiting for transfers between devices, per_device(): lax.psum(jnp.dot(activated, down_w, preferred_element_type=jnp.float32).a...  77.9 us
    reduce_scatter x1, waiting for transfers between devices, per_device(): lax.psum_scatter(grad_list[4], ('dp', 'ctx'), scatter_dimension=1, tiled=...  55.1 us
  transfers between devices with their start and end apart: 19, of which 17 were waited for; matrix products, arithmetic and copies ran while one was open for 9% of the time, Pallas kernels for 0%

profile of v1, /device:TPU:0, one launch (start us, length us, event | category | flops | bytes accessed | tf_op | source)
XLA Modules:
  0.0 1541.1 jit_solution(18199716022214453590)
XLA Ops:
  9.5 10.4 all-gather.4
  22.0 9.8 all_gather.70
  32.9 9.8 all_gather.67
  103.3 9.2 all-gather.5
  112.6 144.4 %all-reduce.12.cloned.1.call-done = (f32[1,256,2048]{2,1,0:T(8,128)}, f32[1,256,2048]{2,1,0:T(8,128)}) async-done(((f32[1,256,2048]{2,1,0:T(8,128)}, f32[1,256,2048]{2,1,0:T(8,128)}), (f32[1,256,2048]{2,1,0:T(8,128)}, f32[1,256,2048]{2,1,0:T(8,128)})) %all-reduce.12.cloned.1.call-update) | async-done | bytes 4194320 | tf_op jit(solution)/shard_map/psum | solution.py:148
  262.7 38.3 %all-gather.18.cloned.1.call-done = bf16[2048,1408]{1,0:T(8,128)(2,1)} async-done(((bf16[256,1408]{1,0:T(8,128)(2,1)}), bf16[2048,1408]{1,0:T(8,128)(2,1)}) %all-gather.18.cloned.1.call-update) | async-done | bytes 5767184 | tf_op jit(solution)/shard_map/all_gather | solution.py:52
  306.5 39.4 %all-gather.20.cloned.1.call-done = bf16[2048,1408]{1,0:T(8,128)(2,1)} async-done(((bf16[256,1408]{1,0:T(8,128)(2,1)}), bf16[2048,1408]{1,0:T(8,128)(2,1)}) %all-gather.20.cloned.1.call-update) | async-done | bytes 5767184 | tf_op jit(solution)/shard_map/all_gather | solution.py:53
  351.4 40.5 %all-gather.22.cloned.1.call-done = bf16[1408,2048]{1,0:T(8,128)(2,1)} async-done(((bf16[1408,256]{1,0:T(8,128)(2,1)}), bf16[1408,2048]{1,0:T(8,128)(2,1)}) %all-gather.22.cloned.1.call-update) | async-done | bytes 5767184 | tf_op jit(solution)/shard_map/all_gather | solution.py:54
  405.6 149.5 %all-gather.24.cloned.1.call-done = f32[1024,2048]{1,0:T(8,128)} async-done(((f32[256,2048]{1,0:T(8,128)}), f32[1024,2048]{1,0:T(8,128)}) %all-gather.24.cloned.1.call-update) | async-done | bytes 8388624 | tf_op jit(solution)/shard_map/all_gather | solution.py:172
  593.1 134.8 %all-gather.26.cloned.1.call-done = f32[1024,2048]{1,0:T(8,128)} async-done(((f32[256,2048]{1,0:T(8,128)}), f32[1024,2048]{1,0:T(8,128)}) %all-gather.26.cloned.1.call-update) | async-done | bytes 8388624 | tf_op jit(solution)/shard_map/all_gather | solution.py:172
  737.4 77.9 %all-reduce.14.cloned.1.call-done = (bf16[1,256,2048]{2,1,0:T(8,128)(2,1)}, bf16[1,256,2048]{2,1,0:T(8,128)(2,1)}) async-done(((bf16[1,256,2048]{2,1,0:T(8,128)(2,1)}, bf16[1,256,2048]{2,1,0:T(8,128)(2,1)}), (bf16[1,256,2048]{2,1,0:T(8,128)(2,1)}, bf16[1,256,2048]{2,1,0:T(8,128)(2,1)})) %all-reduce.14.cloned.1.call-update) | async-done | bytes 2097168 | tf_op jit(solution)/shard_map/psum | solution.py:157
  826.5 8.7 fusion.3
  843.4 8.9 fusion
  889.2 23.9 %reduce-scatter.12.cloned.1.call-done = f32[256,128]{0,1:T(8,128)} async-done(((f32[1024,128]{0,1:T(8,128)}), f32[256,128]{0,1:T(8,128)}) %reduce-scatter.12.cloned.1.call-update) | async-done | bytes 131088 | tf_op jit(solution)/shard_map/reduce_scatter | solution.py:206
  924.2 7.5 fusion.200
  934.0 10.7 convolution_add_fusion.2
  980.1 96.7 %all-reduce.10.cloned.1.call-done = (f32[1,256,2048]{2,1,0:T(8,128)}, f32[1,256,2048]{2,1,0:T(8,128)}) async-done(((f32[1,256,2048]{2,1,0:T(8,128)}, f32[1,256,2048]{2,1,0:T(8,128)}), (f32[1,256,2048]{2,1,0:T(8,128)}, f32[1,256,2048]{2,1,0:T(8,128)})) %all-reduce.10.cloned.1.call-update) | async-done | bytes 4194320 | tf_op jit(solution)/shard_map/psum | solution.py:223
  1080.2 23.9 %all-reduce.2 = (f32[2048]{0:T(1024)S(1)}, f32[2048]{0:T(1024)S(1)}) all-reduce(f32[2048]{0:T(1024)S(1)} %add.250, f32[2048]{0:T(1024)S(1)} %add.255), channel_id=8, replica_groups=mesh['dp'=2,'ctx'=4,'tensor'=4] {'dp','ctx'}, use_global_device_ids=true, to_apply=%region_26.27.clone | all-reduce | flops 4096 | bytes 32768
  1113.7 37.7 %reduce-scatter.18.cloned.1.call-done = f32[256,64]{0,1:T(8,128)} async-done(((f32[2048,64]{0,1:T(8,128)}), f32[256,64]{0,1:T(8,128)}) %reduce-scatter.18.cloned.1.call-update) | async-done | bytes 65552 | tf_op jit(solution)/shard_map/reduce_scatter | solution.py:232
  1151.3 91.1 %reduce-scatter.22.cloned.1.call-done = f32[256,1408]{1,0:T(8,128)} async-done(((f32[2048,1408]{1,0:T(8,128)}), f32[256,1408]{1,0:T(8,128)}) %reduce-scatter.22.cloned.1.call-update) | async-done | bytes 1441808 | tf_op jit(solution)/shard_map/reduce_scatter | solution.py:235
  1242.4 91.1 %reduce-scatter.24.cloned.1.call-done = f32[256,1408]{1,0:T(8,128)} async-done(((f32[2048,1408]{1,0:T(8,128)}), f32[256,1408]{1,0:T(8,128)}) %reduce-scatter.24.cloned.1.call-update) | async-done | bytes 1441808 | tf_op jit(solution)/shard_map/reduce_scatter | solution.py:236
  1333.5 90.8 %reduce-scatter.26.cloned.1.call-done = f32[1408,256]{1,0:T(8,128)} async-done(((f32[1408,2048]{1,0:T(8,128)}), f32[1408,256]{1,0:T(8,128)}) %reduce-scatter.26.cloned.1.call-update) | async-done | bytes 1441808 | tf_op jit(solution)/shard_map/reduce_scatter | solution.py:237
  1424.3 55.0 %reduce-scatter.14.cloned.1.call-done = f32[256,512]{1,0:T(8,128)} async-done(((f32[2048,512]{1,0:T(8,128)}), f32[256,512]{1,0:T(8,128)}) %reduce-scatter.14.cloned.1.call-update) | async-done | bytes 524304 | tf_op jit(solution)/shard_map/reduce_scatter | solution.py:230
  1479.2 55.1 %reduce-scatter.20.cloned.1.call-done = f32[512,256]{1,0:T(8,128)} async-done(((f32[512,2048]{1,0:T(8,128)}), f32[512,256]{1,0:T(8,128)}) %reduce-scatter.20.cloned.1.call-update) | async-done | bytes 524304 | tf_op jit(solution)/shard_map/reduce_scatter | solution.py:233
  (350 shorter events, 259.9 us)
Async XLA Ops:
  7.2 71.8 %all-gather.14.cloned.1.call-start = ((), (), s32[]{:S(2)}) async-start(), calls=%async_computation.9 | async-start | bytes 2359296 | tf_op jit(solution)/shard_map/all_gather | solution.py:47
  7.9 87.7 %all-gather.16.cloned.1.call-start = ((), (), s32[]{:S(2)}) async-start(), calls=%async_computation.10 | async-start | bytes 2359296 | tf_op jit(solution)/shard_map/all_gather | solution.py:50
  8.7 248.3 %all-reduce.12.cloned.1.call-start = ((), (), s32[]{:S(2)}) async-start(), calls=%async_computation.26 | async-start | bytes 8388608 | tf_op jit(solution)/shard_map/psum | solution.py:148
  8.7 35.8 %copy-start.83 = (f32[32]{0:T(128)}, f32[32]{0:T(128)S(1)}, u32[]{:S(2)}) copy-start(f32[32]{0:T(128)S(1)} %multiply_power_fusion) | copy-start | bytes 388
  8.8 35.8 %copy-start.81 = (f32[256]{0:T(256)}, f32[256]{0:T(256)S(1)}, u32[]{:S(2)}) copy-start(f32[256]{0:T(256)S(1)} %fusion.169) | copy-start | bytes 3076
  22.0 60.9 %copy-start.77 = (f32[256]{0:T(256)}, f32[256]{0:T(256)S(1)}, u32[]{:S(2)}) copy-start(f32[256]{0:T(256)S(1)} %add_rsqrt_fusion.3) | copy-start | bytes 3076
  22.0 63.4 %copy-start.79 = (f32[256]{0:T(256)}, f32[256]{0:T(256)S(1)}, u32[]{:S(2)}) copy-start(f32[256]{0:T(256)S(1)} %add_rsqrt_fusion.1) | copy-start | bytes 3076
  101.5 199.4 %all-gather.18.cloned.1.call-start = ((), (), s32[]{:S(2)}) async-start(), calls=%async_computation.11 | async-start | bytes 6488064 | tf_op jit(solution)/shard_map/all_gather | solution.py:52
  102.1 243.8 %all-gather.20.cloned.1.call-start = ((), (), s32[]{:S(2)}) async-start(), calls=%async_computation.12 | async-start | bytes 6488064 | tf_op jit(solution)/shard_map/all_gather | solution.py:53
  102.7 289.2 %all-gather.22.cloned.1.call-start = ((), (), s32[]{:S(2)}) async-start(), calls=%async_computation.13 | async-start | bytes 6488064 | tf_op jit(solution)/shard_map/all_gather | solution.py:54
  103.3 451.9 %all-gather.24.cloned.1.call-start = ((), (), s32[]{:S(2)}) async-start(), calls=%async_computation.23 | async-start | bytes 10485760 | tf_op jit(solution)/shard_map/all_gather | solution.py:172
  262.6 83.3 %copy-start.13 = (bf16[256,2048]{1,0:T(8,128)(2,1)}, bf16[256,2048]{1,0:T(8,128)(2,1)S(1)}, u32[]{:S(2)}) copy-start(bf16[256,2048]{1,0:T(8,128)(2,1)S(1)} %fusion.72) | copy-start | bytes 3145732
  405.4 322.6 %all-gather.26.cloned.1.call-start = ((), (), s32[]{:S(2)}) async-start(), calls=%async_computation.24 | async-start | bytes 10485760 | tf_op jit(solution)/shard_map/all_gather | solution.py:172
  580.0 235.3 %all-reduce.14.cloned.1.call-start = ((), (), s32[]{:S(2)}) async-start(), calls=%async_computation.27 | async-start | bytes 4194304 | tf_op jit(solution)/shard_map/psum | solution.py:157
  592.0 296.4 %reduce-scatter.10.cloned.1.call-start = ((), (), s32[]{:S(2)}) async-start(), calls=%async_computation.14 | async-start | bytes 655360 | tf_op jit(solution)/shard_map/reduce_scatter | solution.py:206
  867.5 45.6 %reduce-scatter.12.cloned.1.call-start = ((), (), s32[]{:S(2)}) async-start(), calls=%async_computation.15 | async-start | bytes 655360 | tf_op jit(solution)/shard_map/reduce_scatter | solution.py:206
  880.4 196.5 %all-reduce.10.cloned.1.call-start = ((), (), s32[]{:S(2)}) async-start(), calls=%async_computation.25 | async-start | bytes 8388608 | tf_op jit(solution)/shard_map/psum | solution.py:223
  921.7 192.0 %reduce-scatter.16.cloned.1.call-start = ((), (), s32[]{:S(2)}) async-start(), calls=%async_computation.17 | async-start | bytes 589824 | tf_op jit(solution)/shard_map/reduce_scatter | solution.py:231
  924.2 227.2 %reduce-scatter.18.cloned.1.call-start = ((), (), s32[]{:S(2)}) async-start(), calls=%async_computation.18 | async-start | bytes 589824 | tf_op jit(solution)/shard_map/reduce_scatter | solution.py:232
  933.9 308.5 %reduce-scatter.22.cloned.1.call-start = ((), (), s32[]{:S(2)}) async-start(), calls=%async_computation.20 | async-start | bytes 12976128 | tf_op jit(solution)/shard_map/reduce_scatter | solution.py:235
  944.7 388.8 %reduce-scatter.24.cloned.1.call-start = ((), (), s32[]{:S(2)}) async-start(), calls=%async_computation.21 | async-start | bytes 12976128 | tf_op jit(solution)/shard_map/reduce_scatter | solution.py:236
  954.4 469.8 %reduce-scatter.26.cloned.1.call-start = ((), (), s32[]{:S(2)}) async-start(), calls=%async_computation.22 | async-start | bytes 12976128 | tf_op jit(solution)/shard_map/reduce_scatter | solution.py:237
  964.6 514.7 %reduce-scatter.14.cloned.1.call-start = ((), (), s32[]{:S(2)}) async-start(), calls=%async_computation.16 | async-start | bytes 4718592 | tf_op jit(solution)/shard_map/reduce_scatter | solution.py:230
  969.3 565.0 %reduce-scatter.20.cloned.1.call-start = ((), (), s32[]{:S(2)}) async-start(), calls=%async_computation.19 | async-start | bytes 4718592 | tf_op jit(solution)/shard_map/reduce_scatter | solution.py:233
  (91 other events, 429.7 us)
Sparse Core Ops, SparseCore 0:
  9.9 31.1 all-gather.13
  43.0 28.4 all-gather.15
  101.6 155.3 all-reduce.11
  258.8 42.1 all-gather.17
  302.7 43.1 all-gather.19
  347.6 44.2 all-gather.21
  405.5 149.5 all-gather.23
  580.1 147.7 all-gather.25
  730.9 84.3 all-reduce.13
  867.7 20.6 reduce-scatter.9
  891.5 21.6 reduce-scatter.11
  921.8 155.0 all-reduce.9
  1080.5 33.0 reduce-scatter.15
  1117.2 34.1 reduce-scatter.17
  1155.2 87.1 reduce-scatter.21
  1246.3 87.1 reduce-scatter.23
  1337.4 86.8 reduce-scatter.25
  1428.1 51.1 reduce-scatter.13
  1483.2 51.0 reduce-scatter.19
